TPU v7x, 32 devices: a whole 2x2x4 slice. The times are simulated.
32 devices in a mesh: cell: 16 (over z, x, core), gene: 2 (over y).
Axes of the slice: x: 2, y: 2, z: 4, core: 2. Of those that a mesh axis runs over, the one named last changes fastest.
Arguments:
- counts: bfloat16 [15360, 16384], P('cell', 'gene'), as said below
- w_factor: float32 [15360, 128], P('cell'), may hold values from 0.004 to 2, as said below
- h_factor: float32 [128, 16384], P('cell', 'gene'), may hold values from 0.03 to 0.3, as said below
Outputs:
- w_updated: float32 [15360, 128], P('cell')
- h_updated: float32 [128, 16384], P('cell', 'gene')
Inputs may be any that keep to these rules, and one draw needn't show every extreme that they name: `counts`: nonnegative whole numbers. `w_factor`: positive. `h_factor`: positive.
All inputs are finite; a program needn't handle non-finite values.
Results may differ from a plain program's by a relative error of at most 0.00092.
Values may be sent and summed in bfloat16 or wider, within the bound.
No kernel may reach another device: no remote copies, remote signals or barrier semaphores. Data moves between devices by JAX's collectives and lax.ppermute only.
A program may use at most 64 MiB of HBM per device.

v0:
```python
import jax
import jax.numpy as jnp
from jax import lax
from jax.sharding import PartitionSpec as P


def per_device(counts, w_factor, h_factor):
    own_rows = h_factor.shape[0]
    rank = w_factor.shape[1]
    w_copy = w_factor.astype(jnp.bfloat16)
    row_offset = lax.axis_index("cell") * own_rows
    counts_float = counts.astype(jnp.float32)
    columns = w_copy
    modeled = jnp.dot(
        columns,
        lax.all_gather(h_factor.astype(jnp.bfloat16), "cell", axis=0, tiled=True),
        preferred_element_type=jnp.float32,
    )
    quotient = (counts_float / modeled).astype(jnp.bfloat16)
    columns = w_copy
    numerator = lax.psum_scatter(
        lax.dot_general(
            columns, quotient, (((0,), (0,)), ((), ())), preferred_element_type=jnp.float32
        ),
        "cell",
        scatter_dimension=0,
        tiled=True,
    )
    w_totals = lax.psum(jnp.sum(w_factor, axis=0), "cell")
    own_totals = lax.dynamic_slice_in_dim(w_totals, row_offset, own_rows, 0)
    h_updated = h_factor * numerator / own_totals[:, None]
    h_new_copy = lax.all_gather(h_updated.astype(jnp.bfloat16), "cell", axis=0, tiled=True)
    modeled_again = jnp.dot(w_copy, h_new_copy, preferred_element_type=jnp.float32)
    quotient_again = (counts_float / modeled_again).astype(jnp.bfloat16)
    partial_w = lax.dot_general(
        quotient_again, h_new_copy, (((1,), (1,)), ((), ())), preferred_element_type=jnp.float32
    )
    partial_totals = jnp.sum(h_new_copy.astype(jnp.float32), axis=1)
    w_share = lax.psum_scatter(partial_w, "gene", scatter_dimension=1, tiled=True)
    h_totals = lax.psum(partial_totals, "gene")
    share_width = rank // lax.axis_size("gene")
    col_offset = lax.axis_index("gene") * share_width
    w_own = lax.dynamic_slice_in_dim(w_factor, col_offset, share_width, 1)
    totals_own = lax.dynamic_slice_in_dim(h_totals, col_offset, share_width, 0)
    w_part = w_own * w_share / totals_own[None, :]
    w_updated = lax.all_gather(w_part, "gene", axis=1, tiled=True)
    return (w_updated, h_updated)


def solution(mesh):
    in_specs = (P("cell", "gene"), P("cell", None), P("cell", "gene"))
    out_specs = (P("cell", None), P("cell", "gene"))
    return jax.shard_map(
        per_device, mesh=mesh, in_specs=in_specs, out_specs=out_specs, check_vma=False
    )
```

profile of v0, /device:TPU:0, one launch (start us, length us, event | category | flops | bytes accessed | tf_op | source)
XLA Modules:
  0.0 248.2 jit_solution(8995357598601707280)
XLA Ops:
  7.2 0.0 all-gather.3.cloned.1.call-start
  7.2 1.6 convert_element_type.23
  8.8 0.0 all-gather.3.cloned.1.call-update
  8.9 0.0 reduce-scatter.7.cloned.1.call-start
  8.9 46.0 %all-gather.3.cloned.1.call-done = bf16[128,8192]{1,0:T(8,128)(2,1)} async-done(((bf16[8,8192]{1,0:T(8,128)(2,1)}), bf16[128,8192]{1,0:T(8,128)(2,1)}) %all-gather.3.cloned.1.call-update) | async-done | bytes 2097168 | tf_op jit(solution)/shard_map/all_gather | solution.py:16
  54.9 16.7 %fusion.4 = f32[128,8192]{0,1:T(8,128)} fusion(bf16[960,8192]{1,0:T(8,128)(2,1)} %param.3, bf16[128,8192]{1,0:T(8,128)(2,1)} %all-gather.3.cloned.1.call-done, f32[960,128]{1,0:T(8,128)} %param.4), kind=kOutput, calls=%fused_computation.5 | convolution fusion | flops 4050370560 | bytes 22511616 | tf_op jit(solution)/shard_map/dot_general | solution.py:22
  71.6 5.6 %copy.14 = f32[128,8192]{1,0:T(8,128)} copy(f32[128,8192]{0,1:T(8,128)} %fusion.4) | data formatting | bytes 8388608
  77.2 0.0 copy-start.2
  77.3 0.0 copy-start.1
  77.3 0.0 reduce-scatter.7.cloned.1.call-update
  77.3 0.0 all-gather.5.cloned.1.call-start
  77.3 0.9 copy-done.2
  78.2 2.6 %copy.10 = f32[8,8192]{0,1:T(8,128)} copy(f32[8,8192]{1,0:T(8,128)S(1)} %copy-done.2) | data formatting | bytes 524288 | tf_op args[2]
  80.8 0.0 copy-done.1
  80.8 0.1 reduce_sum.18
  80.9 31.7 %psum.14 = f32[128]{0:T(128)S(1)} all-reduce(f32[128]{0:T(128)S(1)} %reduce_sum.18), channel_id=1, replica_groups=mesh['cell'=16,'gene'=2] {'cell'}, use_global_device_ids=true, to_apply=%region_2.0 | all-reduce | flops 128 | bytes 1024 | tf_op jit(solution)/shard_map/psum | solution.py:29
  112.6 0.1 dynamic_slice.10
  112.7 36.1 %reduce-scatter.7.cloned.1.call-done = f32[8,8192]{1,0:T(8,128)} async-done(((f32[128,8192]{1,0:T(8,128)}), f32[8,8192]{1,0:T(8,128)}) %reduce-scatter.7.cloned.1.call-update) | async-done | bytes 262160
  148.7 3.5 %copy.15 = f32[8,8192]{0,1:T(8,128)} copy(f32[8,8192]{1,0:T(8,128)} %reduce-scatter.7.cloned.1.call-done) | data formatting | bytes 524288
  152.2 5.9 %fusion.14 = (bf16[8,8192]{0,1:T(8,128)(2,1)S(1)}, f32[8,8192]{0,1:T(8,128)}) fusion(f32[8]{0:T(128)S(1)} %dynamic_slice.10, f32[8,8192]{0,1:T(8,128)} %copy.10, f32[8,8192]{0,1:T(8,128)} %copy.15), kind=kLoop, calls=%fused_computation.14 | loop fusion | flops 196608 | bytes 917536 | tf_op jit(solution)/shard_map/convert_element_type | solution.py:32
  158.1 1.4 copy.11
  159.5 0.0 all-gather.5.cloned.1.call-update
  159.6 0.2 reduce-scatter.5.cloned.1.call-start
  159.8 40.4 %all-gather.5.cloned.1.call-done = bf16[128,8192]{1,0:T(8,128)(2,1)} async-done(((bf16[8,8192]{1,0:T(8,128)(2,1)}), bf16[128,8192]{1,0:T(8,128)(2,1)}) %all-gather.5.cloned.1.call-update) | async-done | bytes 2097168 | tf_op jit(solution)/shard_map/all_gather | solution.py:32
  200.2 17.3 %fusion.9 = f32[960,128]{0,1:T(8,128)} fusion(bf16[128,8192]{1,0:T(8,128)(2,1)} %all-gather.5.cloned.1.call-done, bf16[960,8192]{1,0:T(8,128)(2,1)} %param.3, f32[960,128]{1,0:T(8,128)S(1)} %copy-done.1), kind=kOutput, calls=%fused_computation.7 | convolution fusion | flops 4050247680 | bytes 18808832 | tf_op jit(solution)/shard_map/dot_general | solution.py:35
  217.5 0.0 copy-start
  217.5 0.0 reduce-scatter.5.cloned.1.call-update
  217.5 0.2 constant_dynamic-slice_fusion
  217.7 0.2 copy.16
  217.9 3.7 %copy.13 = f32[8,8192]{1,0:T(8,128)} copy(f32[8,8192]{0,1:T(8,128)} %get-tuple-element.7) | data formatting | bytes 524288
  221.6 0.0 copy-done
  221.6 0.4 convert_reduce_fusion
  221.9 5.1 %psum.15 = f32[128]{0:T(128)S(1)} all-reduce(f32[128]{0:T(128)S(1)} %convert_reduce_fusion), channel_id=1, replica_groups=mesh['cell'=16,'gene'=2] {'gene'}, use_global_device_ids=true, to_apply=%region_5.0 | all-reduce | flops 128 | bytes 1024 | tf_op jit(solution)/shard_map/psum | solution.py:40
  227.1 0.1 dynamic_slice.11
  227.1 4.0 %reduce-scatter.5.cloned.1.call-done = f32[960,64]{0,1:T(8,128)} async-done(((f32[960,128]{0,1:T(8,128)}), f32[960,64]{0,1:T(8,128)}) %reduce-scatter.5.cloned.1.call-update) | async-done | bytes 245776 | tf_op jit(solution)/shard_map/reduce_scatter | solution.py:39
  231.1 1.0 multiply_divide_fusion.1
  232.1 8.5 %all_gather.11 = f32[960,128]{0,1:T(8,128)S(1)} all-gather(f32[960,64]{0,1:T(8,128)S(1)} %multiply_divide_fusion.1), channel_id=1, replica_groups=mesh['cell'=16,'gene'=2] {'gene'}, dimensions={1}, use_global_device_ids=true | all-gather | bytes 737280 | tf_op jit(solution)/shard_map/all_gather | solution.py:46
  240.7 1.0 copy.12
Async XLA Ops:
  7.2 47.8 %all-gather.3.cloned.1.call-start = ((), (), s32[]{:S(2)}) async-start(), calls=%async_computation.2 | async-start | bytes 2228224 | tf_op jit(solution)/shard_map/all_gather | solution.py:16
  8.9 139.9 %reduce-scatter.7.cloned.1.call-start = ((), (), s32[]{:S(2)}) async-start(), calls=%async_computation.5 | async-start | bytes 4456448
  77.2 0.9 copy-start.2
  77.3 3.5 %copy-start.1 = (f32[960,128]{1,0:T(8,128)S(1)}, f32[960,128]{1,0:T(8,128)}, u32[]{:S(2)}) copy-start(f32[960,128]{1,0:T(8,128)} %param.4) | copy-start | bytes 1474564
  77.3 122.9 %all-gather.5.cloned.1.call-start = ((), (), s32[]{:S(2)}) async-start(), calls=%async_computation.3 | async-start | bytes 2228224 | tf_op jit(solution)/shard_map/all_gather | solution.py:32
  159.6 71.5 %reduce-scatter.5.cloned.1.call-start = ((), (), s32[]{:S(2)}) async-start(), calls=%async_computation.4 | async-start | bytes 786432 | tf_op jit(solution)/shard_map/reduce_scatter | solution.py:39
  217.5 4.1 %copy-start = (bf16[128,8192]{1,0:T(8,128)(2,1)S(1)}, bf16[128,8192]{1,0:T(8,128)(2,1)}, u32[]{:S(2)}) copy-start(bf16[128,8192]{1,0:T(8,128)(2,1)} %all-gather.5.cloned.1.call-done) | copy-start | bytes 6291460
Sparse Core Ops, SparseCore 0:
  10.7 44.1 all-gather.2
  77.4 71.2 reduce-scatter.6
  159.7 40.4 all-gather.4
  217.6 13.4 reduce-scatter.4
where the time goes:
time: 249 us; the launch traced here: 248 us
  waiting for transfers between devices  126 us (51%)
  blocking collectives  45.4 us (18%)
  matrix products  34 us (14%)
  local copies, waits for them, and re-layouts  19.2 us (8%)
  between operations  13.8 us (6%)
  other arithmetic  9.09 us (4%)
    all_gather x1, waiting for transfers between devices, per_device(): lax.all_gather(h_factor.astype(jnp.bfloat16), 'cell', axis=0, tiled=True)  46 us
    all_gather x1, waiting for transfers between devices, per_device(): lax.all_gather(h_updated.astype(jnp.bfloat16), 'cell', axis=0, tiled=True)  40.4 us
    unnamed x5, waiting for transfers between devices  36.1 us
    psum x1, blocking collectives, per_device(): w_totals = lax.psum(jnp.sum(w_factor, axis=0), 'cell')  31.7 us
    unnamed x12, local copies, waits for them, and re-layouts  17.4 us
    dot_general x1, matrix products, per_device(): lax.dot_general(quotient_again, h_new_copy, (((1,), (1,)), ((), ())), pre...  17.3 us
    dot_general x1, matrix products, per_device(): lax.dot_general(columns, quotient, (((0,), (0,)), ((), ())), preferred_el...  16.7 us
    all_gather x1, blocking collectives, per_device(): w_updated = lax.all_gather(w_part, 'gene', axis=1, tiled=True)  8.55 us
  transfers between devices with their start and end apart: 4, of which 4 were waited for; matrix products, arithmetic and copies ran while one was open for 3% of the time, Pallas kernels for 0%

commit v1 on v0

--- a/solution.py
+++ b/solution.py
@@ -1,7 +1,36 @@
+import functools
 import jax
 import jax.numpy as jnp
 from jax import lax
 from jax.sharding import PartitionSpec as P
+
+
+def figure_remake(payload, dim_no):
+    v1 = lax.axis_index("cell")
+    seen_now = lax.axis_size("cell")
+    all_values, b_next, t1 = (seen_now, v1, payload.shape[dim_no])
+    sides = tuple(
+        (to_i * all_values if d == dim_no else to_i for d, to_i in enumerate(payload.shape))
+    )
+    raw_out = jnp.zeros(sides, payload.dtype)
+    odd = now = payload
+    placed = lax.dynamic_update_slice_in_dim(raw_out, payload, b_next * t1, axis=dim_no)
+    for dev_i in range(1, all_values // 2 + 1):
+        t_next = tuple(((d, (d + 1) % all_values) for d in range(all_values)))
+        odd = lax.ppermute(odd, "cell", t_next)
+        placed = lax.dynamic_update_slice_in_dim(
+            placed, odd, (b_next - dev_i) % all_values * t1, axis=dim_no
+        )
+        if 2 * dev_i < all_values:
+            response = tuple(((d, (d - 1) % all_values) for d in range(all_values)))
+            now = lax.ppermute(now, "cell", response)
+            placed = lax.dynamic_update_slice_in_dim(
+                placed, now, (b_next + dev_i) % all_values * t1, axis=dim_no
+            )
+    return placed
+
+
+attach_roots = functools.partial(figure_remake, dim_no=0)
 
 
 def per_device(counts, w_factor, h_factor):
@@ -12,9 +41,7 @@
     counts_float = counts.astype(jnp.float32)
     columns = w_copy
     modeled = jnp.dot(
-        columns,
-        lax.all_gather(h_factor.astype(jnp.bfloat16), "cell", axis=0, tiled=True),
-        preferred_element_type=jnp.float32,
+        columns, attach_roots(h_factor.astype(jnp.bfloat16)), preferred_element_type=jnp.float32
     )
     quotient = (counts_float / modeled).astype(jnp.bfloat16)
     columns = w_copy

time: 249 us -> 256 us (1.028)
  starting transfers between devices: 0.34 us -> 32.6 us
  waiting for transfers between devices: 126 us -> 108 us
  matrix products: 34 us -> 31.1 us
    all_gather x1 -> x0, waiting for transfers between devices: 46 us -> none  [per_device(): lax.all_gather(h_factor.astype(jnp.bfloat16), 'cell', axis=0, tiled=True)]
    ppermute x0 -> x15, starting transfers between devices: none -> 32.3 us  [the longest x7 31.8 us: figure_remake(): now = lax.ppermute(now, 'cell', response)]
    ppermute x0 -> x15, waiting for transfers between devices: none -> 25.7 us  [the longest x8 25.6 us: figure_remake(): odd = lax.ppermute(odd, 'cell', t_next)]
    dot_general x1, matrix products: 16.7 us -> 13.8 us  [per_device(): lax.dot_general(columns, quotient, (((0,), (0,)), ((), ())), preferred_el...]
    unnamed x5 -> x4, waiting for transfers between devices: 36.1 us -> 38.1 us
  transfers between devices with their start and end apart: 4 -> 18, of which waited for: 4 -> 11; matrix products, arithmetic and copies ran while one was open for 3% -> 3% of each run, Pallas kernels for 0% -> 0%
where the time goes in v1:
time: 256 us
  waiting for transfers between devices  108 us (42%)
  blocking collectives  43.4 us (17%)
  starting transfers between devices  32.6 us (13%)
  matrix products  31.1 us (12%)
  local copies, waits for them, and re-layouts  19.3 us (8%)
  between operations  13.9 us (5%)
  other arithmetic  7.52 us (3%)
    all_gather x1, waiting for transfers between devices, per_device(): lax.all_gather(h_updated.astype(jnp.bfloat16), 'cell', axis=0, tiled=True)  40.5 us
    unnamed x4, waiting for transfers between devices  38.1 us
    ppermute x7, starting transfers between devices, figure_remake(): now = lax.ppermute(now, 'cell', response)  31.8 us
    psum x1, blocking collectives, per_device(): w_totals = lax.psum(jnp.sum(w_factor, axis=0), 'cell')  29.7 us
    ppermute x8, waiting for transfers between devices, figure_remake(): odd = lax.ppermute(odd, 'cell', t_next)  25.6 us
    dot_general x1, matrix products, per_device(): lax.dot_general(quotient_again, h_new_copy, (((1,), (1,)), ((), ())), pre...  17.3 us
    unnamed x12, local copies, waits for them, and re-layouts  17.2 us
    dot_general x1, matrix products, per_device(): lax.dot_general(columns, quotient, (((0,), (0,)), ((), ())), preferred_el...  13.8 us
  transfers between devices with their start and end apart: 18, of which 11 were waited for; matrix products, arithmetic and copies ran while one was open for 3% of the time, Pallas kernels for 0%

profile of v1, /device:TPU:0, one launch (start us, length us, event | category | flops | bytes accessed | tf_op | source)
XLA Modules:
  0.0 256.1 jit_solution(2317339135928164540)
XLA Ops:
  7.2 0.0 reduce-scatter.7.cloned.1.call-start
  7.2 0.2 broadcast_in_dim.2
  7.4 0.7 copy-done.2
  8.1 0.5 collective-permute-start
  8.7 5.0 %collective-permute-start.1 = (bf16[8,8192]{1,0:T(8,128)(2,1)S(1)}, bf16[8,8192]{1,0:T(8,128)(2,1)S(1)}, u32[]{:S(2)}, u32[]{:S(2)}) collective-permute-start(bf16[8,8192]{1,0:T(8,128)(2,1)S(1)} %get-tuple-element.9), channel_id=1, source_target_pairs={{0,30},{2,0},{4,2},{6,4},{8,6},{10,8},{12,10},{14,12},{16,14},{18,... | collective-permute-start | bytes 393224 | tf_op jit(solution)/shard_map/ppermute | solution.py:26
  13.7 2.7 %collective-permute-done = bf16[8,8192]{1,0:T(8,128)(2,1)S(1)} collective-permute-done((bf16[8,8192]{1,0:T(8,128)(2,1)S(1)}, bf16[8,8192]{1,0:T(8,128)(2,1)S(1)}, u32[]{:S(2)}, u32[]{:S(2)}) %collective-permute-start) | collective-permute-done | bytes 131104 | tf_op jit(solution)/shard_map/ppermute | solution.py:20
  16.4 0.0 collective-permute-start.2
  16.4 0.0 collective-permute-done.1
  16.4 4.4 %collective-permute-start.3 = (bf16[8,8192]{1,0:T(8,128)(2,1)S(1)}, bf16[8,8192]{1,0:T(8,128)(2,1)S(1)}, u32[]{:S(2)}, u32[]{:S(2)}) collective-permute-start(bf16[8,8192]{1,0:T(8,128)(2,1)S(1)} %collective-permute-done.1), channel_id=1, source_target_pairs={{0,30},{2,0},{4,2},{6,4},{8,6},{10,8},{12,10},{14,12},{16,14},{18,... | collective-permute-start | bytes 393224 | tf_op jit(solution)/shard_map/ppermute | solution.py:26
  20.9 2.6 %collective-permute-done.2 = bf16[8,8192]{1,0:T(8,128)(2,1)S(1)} collective-permute-done((bf16[8,8192]{1,0:T(8,128)(2,1)S(1)}, bf16[8,8192]{1,0:T(8,128)(2,1)S(1)}, u32[]{:S(2)}, u32[]{:S(2)}) %collective-permute-start.2) | collective-permute-done | bytes 131104 | tf_op jit(solution)/shard_map/ppermute | solution.py:20
  23.5 4.5 %collective-permute-start.5 = (bf16[8,8192]{1,0:T(8,128)(2,1)S(1)}, bf16[8,8192]{1,0:T(8,128)(2,1)S(1)}, u32[]{:S(2)}, u32[]{:S(2)}) collective-permute-start(bf16[8,8192]{1,0:T(8,128)(2,1)S(1)} %collective-permute-done.3), channel_id=1, source_target_pairs={{0,30},{2,0},{4,2},{6,4},{8,6},{10,8},{12,10},{14,12},{16,14},{18,... | collective-permute-start | bytes 393224 | tf_op jit(solution)/shard_map/ppermute | solution.py:26
  28.1 2.6 %collective-permute-done.4 = bf16[8,8192]{1,0:T(8,128)(2,1)S(1)} collective-permute-done((bf16[8,8192]{1,0:T(8,128)(2,1)S(1)}, bf16[8,8192]{1,0:T(8,128)(2,1)S(1)}, u32[]{:S(2)}, u32[]{:S(2)}) %collective-permute-start.4) | collective-permute-done | bytes 131104 | tf_op jit(solution)/shard_map/ppermute | solution.py:20
  30.7 4.4 %collective-permute-start.7 = (bf16[8,8192]{1,0:T(8,128)(2,1)S(1)}, bf16[8,8192]{1,0:T(8,128)(2,1)S(1)}, u32[]{:S(2)}, u32[]{:S(2)}) collective-permute-start(bf16[8,8192]{1,0:T(8,128)(2,1)S(1)} %collective-permute-done.5), channel_id=1, source_target_pairs={{0,30},{2,0},{4,2},{6,4},{8,6},{10,8},{12,10},{14,12},{16,14},{18,... | collective-permute-start | bytes 393224 | tf_op jit(solution)/shard_map/ppermute | solution.py:26
  35.2 2.7 %collective-permute-done.6 = bf16[8,8192]{1,0:T(8,128)(2,1)S(1)} collective-permute-done((bf16[8,8192]{1,0:T(8,128)(2,1)S(1)}, bf16[8,8192]{1,0:T(8,128)(2,1)S(1)}, u32[]{:S(2)}, u32[]{:S(2)}) %collective-permute-start.6) | collective-permute-done | bytes 131104 | tf_op jit(solution)/shard_map/ppermute | solution.py:20
  37.9 4.4 %collective-permute-start.9 = (bf16[8,8192]{1,0:T(8,128)(2,1)S(1)}, bf16[8,8192]{1,0:T(8,128)(2,1)S(1)}, u32[]{:S(2)}, u32[]{:S(2)}) collective-permute-start(bf16[8,8192]{1,0:T(8,128)(2,1)S(1)} %collective-permute-done.7), channel_id=1, source_target_pairs={{0,30},{2,0},{4,2},{6,4},{8,6},{10,8},{12,10},{14,12},{16,14},{18,... | collective-permute-start | bytes 393224 | tf_op jit(solution)/shard_map/ppermute | solution.py:26
  42.4 2.7 %collective-permute-done.8 = bf16[8,8192]{1,0:T(8,128)(2,1)S(1)} collective-permute-done((bf16[8,8192]{1,0:T(8,128)(2,1)S(1)}, bf16[8,8192]{1,0:T(8,128)(2,1)S(1)}, u32[]{:S(2)}, u32[]{:S(2)}) %collective-permute-start.8) | collective-permute-done | bytes 131104 | tf_op jit(solution)/shard_map/ppermute | solution.py:20
  45.1 4.4 %collective-permute-start.11 = (bf16[8,8192]{1,0:T(8,128)(2,1)S(1)}, bf16[8,8192]{1,0:T(8,128)(2,1)S(1)}, u32[]{:S(2)}, u32[]{:S(2)}) collective-permute-start(bf16[8,8192]{1,0:T(8,128)(2,1)S(1)} %collective-permute-done.9), channel_id=1, source_target_pairs={{0,30},{2,0},{4,2},{6,4},{8,6},{10,8},{12,10},{14,12},{16,14},{18,... | collective-permute-start | bytes 393224 | tf_op jit(solution)/shard_map/ppermute | solution.py:26
  49.5 2.7 %collective-permute-done.10 = bf16[8,8192]{1,0:T(8,128)(2,1)S(1)} collective-permute-done((bf16[8,8192]{1,0:T(8,128)(2,1)S(1)}, bf16[8,8192]{1,0:T(8,128)(2,1)S(1)}, u32[]{:S(2)}, u32[]{:S(2)}) %collective-permute-start.10) | collective-permute-done | bytes 131104 | tf_op jit(solution)/shard_map/ppermute | solution.py:20
  52.3 4.4 %collective-permute-start.13 = (bf16[8,8192]{1,0:T(8,128)(2,1)S(1)}, bf16[8,8192]{1,0:T(8,128)(2,1)S(1)}, u32[]{:S(2)}, u32[]{:S(2)}) collective-permute-start(bf16[8,8192]{1,0:T(8,128)(2,1)S(1)} %collective-permute-done.11), channel_id=1, source_target_pairs={{0,30},{2,0},{4,2},{6,4},{8,6},{10,8},{12,10},{14,12},{16,14},{18,... | collective-permute-start | bytes 393224 | tf_op jit(solution)/shard_map/ppermute | solution.py:26
  56.7 2.6 %collective-permute-done.12 = bf16[8,8192]{1,0:T(8,128)(2,1)S(1)} collective-permute-done((bf16[8,8192]{1,0:T(8,128)(2,1)S(1)}, bf16[8,8192]{1,0:T(8,128)(2,1)S(1)}, u32[]{:S(2)}, u32[]{:S(2)}) %collective-permute-start.12) | collective-permute-done | bytes 131104 | tf_op jit(solution)/shard_map/ppermute | solution.py:20
  59.4 7.0 %collective-permute-done.14 = bf16[8,8192]{1,0:T(8,128)(2,1)S(1)} collective-permute-done((bf16[8,8192]{1,0:T(8,128)(2,1)S(1)}, bf16[8,8192]{1,0:T(8,128)(2,1)S(1)}, u32[]{:S(2)}, u32[]{:S(2)}) %collective-permute-start.14) | collective-permute-done | bytes 131104 | tf_op jit(solution)/shard_map/ppermute | solution.py:20
  66.5 13.8 %convolution_bitcast_fusion = f32[128,8192]{0,1:T(8,128)} fusion(bf16[960,8192]{1,0:T(8,128)(2,1)} %param.3, bf16[128,8192]{1,0:T(8,128)(2,1)S(1)} %constant_dynamic-update-slice_fusion, f32[960,128]{1,0:T(8,128)S(1)} %copy-done.1), kind=kOutput, calls=%fused_computation.4 | convolution fusion | flops 4050370560 | bytes 22511616 | tf_op jit(solution)/shard_map/dot_general | solution.py:49
  80.3 5.6 %copy.14 = f32[128,8192]{1,0:T(8,128)} copy(f32[128,8192]{0,1:T(8,128)} %convolution_bitcast_fusion) | data formatting | bytes 8388608
  85.9 0.0 reduce-scatter.7.cloned.1.call-update
  85.9 0.0 all-gather.2.cloned.1.call-start
  86.0 2.6 %copy.10 = f32[8,8192]{0,1:T(8,128)} copy(f32[8,8192]{1,0:T(8,128)S(1)} %copy-done.2) | data formatting | bytes 524288 | tf_op args[2]
  88.6 0.1 reduce_sum.18
  88.7 29.7 %psum.14 = f32[128]{0:T(128)S(1)} all-reduce(f32[128]{0:T(128)S(1)} %reduce_sum.18), channel_id=1, replica_groups=mesh['cell'=16,'gene'=2] {'cell'}, use_global_device_ids=true, to_apply=%region_2.3 | all-reduce | flops 128 | bytes 1024 | tf_op jit(solution)/shard_map/psum | solution.py:56
  118.4 0.1 dynamic_slice.10
  118.5 38.0 %reduce-scatter.7.cloned.1.call-done = f32[8,8192]{1,0:T(8,128)} async-done(((f32[128,8192]{1,0:T(8,128)}), f32[8,8192]{1,0:T(8,128)}) %reduce-scatter.7.cloned.1.call-update) | async-done | bytes 262160
  156.5 3.5 %copy.15 = f32[8,8192]{0,1:T(8,128)} copy(f32[8,8192]{1,0:T(8,128)} %reduce-scatter.7.cloned.1.call-done) | data formatting | bytes 524288
  160.0 6.0 %fusion.7 = (bf16[8,8192]{0,1:T(8,128)(2,1)S(1)}, f32[8,8192]{0,1:T(8,128)}) fusion(f32[8]{0:T(128)S(1)} %dynamic_slice.10, f32[8,8192]{0,1:T(8,128)} %copy.10, f32[8,8192]{0,1:T(8,128)} %copy.15), kind=kLoop, calls=%fused_computation.28 | loop fusion | flops 196608 | bytes 917536 | tf_op jit(solution)/shard_map/convert_element_type | solution.py:59
  166.0 1.4 copy.11
  167.4 0.0 all-gather.2.cloned.1.call-update
  167.4 0.2 reduce-scatter.5.cloned.1.call-start
  167.6 40.5 %all-gather.2.cloned.1.call-done = bf16[128,8192]{1,0:T(8,128)(2,1)} async-done(((bf16[8,8192]{1,0:T(8,128)(2,1)}), bf16[128,8192]{1,0:T(8,128)(2,1)}) %all-gather.2.cloned.1.call-update) | async-done | bytes 2097168 | tf_op jit(solution)/shard_map/all_gather | solution.py:59
  208.1 17.3 %fusion.2 = f32[960,128]{0,1:T(8,128)} fusion(bf16[128,8192]{1,0:T(8,128)(2,1)} %all-gather.2.cloned.1.call-done, bf16[960,8192]{1,0:T(8,128)(2,1)} %param.3, f32[960,128]{1,0:T(8,128)S(1)} %copy-done.1), kind=kOutput, calls=%fused_computation.5 | convolution fusion | flops 4050247680 | bytes 18808832 | tf_op jit(solution)/shard_map/dot_general | solution.py:62
  225.4 0.0 reduce-scatter.5.cloned.1.call-update
  225.4 0.2 constant_dynamic-slice_fusion
  225.6 0.2 copy.16
  225.8 3.6 %copy.13 = f32[8,8192]{1,0:T(8,128)} copy(f32[8,8192]{0,1:T(8,128)} %get-tuple-element.7) | data formatting | bytes 524288
  229.4 0.4 convert_reduce_fusion
  229.8 5.1 %psum.15 = f32[128]{0:T(128)S(1)} all-reduce(f32[128]{0:T(128)S(1)} %convert_reduce_fusion), channel_id=1, replica_groups=mesh['cell'=16,'gene'=2] {'gene'}, use_global_device_ids=true, to_apply=%region_5.6 | all-reduce | flops 128 | bytes 1024 | tf_op jit(solution)/shard_map/psum | solution.py:67
  234.9 0.1 dynamic_slice.11
  235.0 4.0 %reduce-scatter.5.cloned.1.call-done = f32[960,64]{0,1:T(8,128)} async-done(((f32[960,128]{0,1:T(8,128)}), f32[960,64]{0,1:T(8,128)}) %reduce-scatter.5.cloned.1.call-update) | async-done | bytes 245776 | tf_op jit(solution)/shard_map/reduce_scatter | solution.py:66
  239.0 1.0 multiply_divide_fusion.1
  240.1 8.5 %all_gather.7 = f32[960,128]{0,1:T(8,128)S(1)} all-gather(f32[960,64]{0,1:T(8,128)S(1)} %multiply_divide_fusion.1), channel_id=1, replica_groups=mesh['cell'=16,'gene'=2] {'gene'}, dimensions={1}, use_global_device_ids=true | all-gather | bytes 737280 | tf_op jit(solution)/shard_map/all_gather | solution.py:73
  248.6 1.0 copy.12
  (33 shorter events, 0.3 us)
Async XLA Ops:
  7.2 1.0 copy-start.2
  7.2 149.3 %reduce-scatter.7.cloned.1.call-start = ((), (), s32[]{:S(2)}) async-start(), calls=%async_computation.4 | async-start | bytes 4456448
  8.1 8.3 %collective-permute-start = (bf16[8,8192]{1,0:T(8,128)(2,1)S(1)}, bf16[8,8192]{1,0:T(8,128)(2,1)S(1)}, u32[]{:S(2)}, u32[]{:S(2)}) collective-permute-start(bf16[8,8192]{1,0:T(8,128)(2,1)S(1)} %get-tuple-element.9), channel_id=1, source_target_pairs={{0,2},{2,4},{4,6},{6,8},{8,10},{10,12},{12,14},{14,16},{16,18},{18... | collective-permute-start | bytes 393224 | tf_op jit(solution)/shard_map/ppermute | solution.py:20
  8.7 7.7 %collective-permute-start.1 = (bf16[8,8192]{1,0:T(8,128)(2,1)S(1)}, bf16[8,8192]{1,0:T(8,128)(2,1)S(1)}, u32[]{:S(2)}, u32[]{:S(2)}) collective-permute-start(bf16[8,8192]{1,0:T(8,128)(2,1)S(1)} %get-tuple-element.9), channel_id=1, source_target_pairs={{0,30},{2,0},{4,2},{6,4},{8,6},{10,8},{12,10},{14,12},{16,14},{18,... | collective-permute-start | bytes 393224 | tf_op jit(solution)/shard_map/ppermute | solution.py:26
  13.7 52.7 %copy-start.1 = (f32[960,128]{1,0:T(8,128)S(1)}, f32[960,128]{1,0:T(8,128)}, u32[]{:S(2)}) copy-start(f32[960,128]{1,0:T(8,128)} %param.4) | copy-start | bytes 1474564
  16.4 7.1 %collective-permute-start.2 = (bf16[8,8192]{1,0:T(8,128)(2,1)S(1)}, bf16[8,8192]{1,0:T(8,128)(2,1)S(1)}, u32[]{:S(2)}, u32[]{:S(2)}) collective-permute-start(bf16[8,8192]{1,0:T(8,128)(2,1)S(1)} %collective-permute-done), channel_id=1, source_target_pairs={{0,2},{2,4},{4,6},{6,8},{8,10},{10,12},{12,14},{14,16},{16,18},{18... | collective-permute-start | bytes 393224 | tf_op jit(solution)/shard_map/ppermute | solution.py:20
  16.4 7.1 %collective-permute-start.3 = (bf16[8,8192]{1,0:T(8,128)(2,1)S(1)}, bf16[8,8192]{1,0:T(8,128)(2,1)S(1)}, u32[]{:S(2)}, u32[]{:S(2)}) collective-permute-start(bf16[8,8192]{1,0:T(8,128)(2,1)S(1)} %collective-permute-done.1), channel_id=1, source_target_pairs={{0,30},{2,0},{4,2},{6,4},{8,6},{10,8},{12,10},{14,12},{16,14},{18,... | collective-permute-start | bytes 393224 | tf_op jit(solution)/shard_map/ppermute | solution.py:26
  23.5 7.2 %collective-permute-start.4 = (bf16[8,8192]{1,0:T(8,128)(2,1)S(1)}, bf16[8,8192]{1,0:T(8,128)(2,1)S(1)}, u32[]{:S(2)}, u32[]{:S(2)}) collective-permute-start(bf16[8,8192]{1,0:T(8,128)(2,1)S(1)} %collective-permute-done.2), channel_id=1, source_target_pairs={{0,2},{2,4},{4,6},{6,8},{8,10},{10,12},{12,14},{14,16},{16,18},{18... | collective-permute-start | bytes 393224 | tf_op jit(solution)/shard_map/ppermute | solution.py:20
  23.5 7.2 %collective-permute-start.5 = (bf16[8,8192]{1,0:T(8,128)(2,1)S(1)}, bf16[8,8192]{1,0:T(8,128)(2,1)S(1)}, u32[]{:S(2)}, u32[]{:S(2)}) collective-permute-start(bf16[8,8192]{1,0:T(8,128)(2,1)S(1)} %collective-permute-done.3), channel_id=1, source_target_pairs={{0,30},{2,0},{4,2},{6,4},{8,6},{10,8},{12,10},{14,12},{16,14},{18,... | collective-permute-start | bytes 393224 | tf_op jit(solution)/shard_map/ppermute | solution.py:26
  30.7 7.2 %collective-permute-start.6 = (bf16[8,8192]{1,0:T(8,128)(2,1)S(1)}, bf16[8,8192]{1,0:T(8,128)(2,1)S(1)}, u32[]{:S(2)}, u32[]{:S(2)}) collective-permute-start(bf16[8,8192]{1,0:T(8,128)(2,1)S(1)} %collective-permute-done.4), channel_id=1, source_target_pairs={{0,2},{2,4},{4,6},{6,8},{8,10},{10,12},{12,14},{14,16},{16,18},{18... | collective-permute-start | bytes 393224 | tf_op jit(solution)/shard_map/ppermute | solution.py:20
  30.7 7.2 %collective-permute-start.7 = (bf16[8,8192]{1,0:T(8,128)(2,1)S(1)}, bf16[8,8192]{1,0:T(8,128)(2,1)S(1)}, u32[]{:S(2)}, u32[]{:S(2)}) collective-permute-start(bf16[8,8192]{1,0:T(8,128)(2,1)S(1)} %collective-permute-done.5), channel_id=1, source_target_pairs={{0,30},{2,0},{4,2},{6,4},{8,6},{10,8},{12,10},{14,12},{16,14},{18,... | collective-permute-start | bytes 393224 | tf_op jit(solution)/shard_map/ppermute | solution.py:26
  37.9 7.2 %collective-permute-start.8 = (bf16[8,8192]{1,0:T(8,128)(2,1)S(1)}, bf16[8,8192]{1,0:T(8,128)(2,1)S(1)}, u32[]{:S(2)}, u32[]{:S(2)}) collective-permute-start(bf16[8,8192]{1,0:T(8,128)(2,1)S(1)} %collective-permute-done.6), channel_id=1, source_target_pairs={{0,2},{2,4},{4,6},{6,8},{8,10},{10,12},{12,14},{14,16},{16,18},{18... | collective-permute-start | bytes 393224 | tf_op jit(solution)/shard_map/ppermute | solution.py:20
  37.9 7.2 %collective-permute-start.9 = (bf16[8,8192]{1,0:T(8,128)(2,1)S(1)}, bf16[8,8192]{1,0:T(8,128)(2,1)S(1)}, u32[]{:S(2)}, u32[]{:S(2)}) collective-permute-start(bf16[8,8192]{1,0:T(8,128)(2,1)S(1)} %collective-permute-done.7), channel_id=1, source_target_pairs={{0,30},{2,0},{4,2},{6,4},{8,6},{10,8},{12,10},{14,12},{16,14},{18,... | collective-permute-start | bytes 393224 | tf_op jit(solution)/shard_map/ppermute | solution.py:26
  45.1 7.2 %collective-permute-start.10 = (bf16[8,8192]{1,0:T(8,128)(2,1)S(1)}, bf16[8,8192]{1,0:T(8,128)(2,1)S(1)}, u32[]{:S(2)}, u32[]{:S(2)}) collective-permute-start(bf16[8,8192]{1,0:T(8,128)(2,1)S(1)} %collective-permute-done.8), channel_id=1, source_target_pairs={{0,2},{2,4},{4,6},{6,8},{8,10},{10,12},{12,14},{14,16},{16,18},{18... | collective-permute-start | bytes 393224 | tf_op jit(solution)/shard_map/ppermute | solution.py:20
  45.1 7.2 %collective-permute-start.11 = (bf16[8,8192]{1,0:T(8,128)(2,1)S(1)}, bf16[8,8192]{1,0:T(8,128)(2,1)S(1)}, u32[]{:S(2)}, u32[]{:S(2)}) collective-permute-start(bf16[8,8192]{1,0:T(8,128)(2,1)S(1)} %collective-permute-done.9), channel_id=1, source_target_pairs={{0,30},{2,0},{4,2},{6,4},{8,6},{10,8},{12,10},{14,12},{16,14},{18,... | collective-permute-start | bytes 393224 | tf_op jit(solution)/shard_map/ppermute | solution.py:26
  52.2 7.1 %collective-permute-start.12 = (bf16[8,8192]{1,0:T(8,128)(2,1)S(1)}, bf16[8,8192]{1,0:T(8,128)(2,1)S(1)}, u32[]{:S(2)}, u32[]{:S(2)}) collective-permute-start(bf16[8,8192]{1,0:T(8,128)(2,1)S(1)} %collective-permute-done.10), channel_id=1, source_target_pairs={{0,2},{2,4},{4,6},{6,8},{8,10},{10,12},{12,14},{14,16},{16,18},{18... | collective-permute-start | bytes 393224 | tf_op jit(solution)/shard_map/ppermute | solution.py:20
  52.3 7.1 %collective-permute-start.13 = (bf16[8,8192]{1,0:T(8,128)(2,1)S(1)}, bf16[8,8192]{1,0:T(8,128)(2,1)S(1)}, u32[]{:S(2)}, u32[]{:S(2)}) collective-permute-start(bf16[8,8192]{1,0:T(8,128)(2,1)S(1)} %collective-permute-done.11), channel_id=1, source_target_pairs={{0,30},{2,0},{4,2},{6,4},{8,6},{10,8},{12,10},{14,12},{16,14},{18,... | collective-permute-start | bytes 393224 | tf_op jit(solution)/shard_map/ppermute | solution.py:26
  59.3 7.1 %collective-permute-start.14 = (bf16[8,8192]{1,0:T(8,128)(2,1)S(1)}, bf16[8,8192]{1,0:T(8,128)(2,1)S(1)}, u32[]{:S(2)}, u32[]{:S(2)}) collective-permute-start(bf16[8,8192]{1,0:T(8,128)(2,1)S(1)} %collective-permute-done.12), channel_id=1, source_target_pairs={{0,2},{2,4},{4,6},{6,8},{8,10},{10,12},{12,14},{14,16},{16,18},{18... | collective-permute-start | bytes 393224 | tf_op jit(solution)/shard_map/ppermute | solution.py:20
  85.9 122.2 %all-gather.2.cloned.1.call-start = ((), (), s32[]{:S(2)}) async-start(), calls=%async_computation.2 | async-start | bytes 2228224 | tf_op jit(solution)/shard_map/all_gather | solution.py:59
  167.4 71.6 %reduce-scatter.5.cloned.1.call-start = ((), (), s32[]{:S(2)}) async-start(), calls=%async_computation.3 | async-start | bytes 786432 | tf_op jit(solution)/shard_map/reduce_scatter | solution.py:66
  225.8 3.6 %copy-start = (bf16[128,8192]{1,0:T(8,128)(2,1)S(1)}, bf16[128,8192]{1,0:T(8,128)(2,1)}, u32[]{:S(2)}) copy-start(bf16[128,8192]{1,0:T(8,128)(2,1)} %all-gather.2.cloned.1.call-done) | copy-start | bytes 6291460
Sparse Core Ops, SparseCore 0:
  86.0 70.4 reduce-scatter.6
  167.5 40.5 all-gather.1
  225.6 13.4 reduce-scatter.4
